TPU v7x, 256 devices: a whole 4x4x8 slice. The times are simulated.
256 devices in a mesh: ctx: 16 (over x, y_hi, core), grp: 16 (over y_lo, z).
Axes of the slice: x: 4, y: 4 (y_hi: 2, y_lo: 2; y = y_hi * 2 + y_lo), z: 8, core: 2. Of those that a mesh axis runs over, the one named last changes fastest.
Arguments:
- tokens: bfloat16 [65536, 2560], P(('ctx', 'grp')), may hold values from -6 to 6
- norm_gain: bfloat16 [2560], replicated, may hold values from 0.5 to 1.5
- w_query: bfloat16 [2560, 2560], P('grp'), may hold values from -0.125 to 0.125
- w_key: bfloat16 [2560, 512], P('grp'), may hold values from -0.125 to 0.125
- w_value: bfloat16 [2560, 512], P('grp'), may hold values from -0.125 to 0.125
- b_query: bfloat16 [2560], replicated, may hold values from -3 to 3
- b_key: bfloat16 [512], replicated, may hold values from -3 to 3
- b_value: bfloat16 [512], replicated, may hold values from -3 to 3
- cache_keys: bfloat16 [2048, 512], P('ctx'), may hold values from -140 to 140
- cache_values: bfloat16 [2048, 512], P('ctx'), may hold values from -6 to 6
- block_lists: int32 [20, 512, 4], P(None, ('ctx', 'grp')), may hold values from -1 to 15, as said below
- start_position: int32 [1], replicated, may hold values from 0 to 983040
Outputs:
- context: float32 [65536, 2560], P(('ctx', 'grp'))
- keys_new: float32 [65536, 512], P(('ctx', 'grp'))
- values_new: float32 [65536, 512], P(('ctx', 'grp'))
Inputs may be any that keep to these rules, and one draw needn't show every extreme that they name: `block_lists`: each list names distinct blocks of 128 prefix positions, named blocks first and -1 in the empty slots after them; every list names at least one block, some list names 4 and some only one.
All inputs are finite; a program needn't handle non-finite values.
Results may differ from a plain program's by a relative error of at most 0.034.
Values may be sent and summed in bfloat16 or wider, within the bound.
A program may use at most 128 MiB of HBM per device.

v0:
```python
import jax
import jax.numpy as jnp
import numpy as np
from jax import lax
from jax.sharding import PartitionSpec as P

HD = 128
GROUP = 5
QBLK = 128
norm_eps = 1e-06
rope_base = 10000000.0


def angle_tables(head_dim):
    half_dim = head_dim // 2
    frequency = rope_base ** (-2.0 * np.arange(half_dim) / head_dim)
    return np.stack(
        [np.mod(frequency * 32.0**digit_level, 2.0 * np.pi) for digit_level in range(4)]
    )


def rotate(values, positions):
    head_dim = values.shape[-1]
    half_dim = head_dim // 2
    tables = jnp.asarray(angle_tables(head_dim), jnp.float32)
    angles = jnp.zeros((positions.shape[0], half_dim), jnp.float32)
    remaining = positions
    for digit_level in range(4):
        digit_value = (remaining % 32).astype(jnp.float32)
        angles = angles + digit_value[:, None] * tables[digit_level][None, :]
        remaining = remaining // 32
    cosine = jnp.cos(angles)[:, None, :]
    sine_part = jnp.sin(angles)[:, None, :]
    lower_half = values[..., :half_dim]
    upper_half = values[..., half_dim:]
    return jnp.concatenate(
        [
            lower_half * cosine - upper_half * sine_part,
            upper_half * cosine + lower_half * sine_part,
        ],
        axis=-1,
    )


def on_device(
    tokens,
    norm_gain,
    w_query,
    w_key,
    w_value,
    b_query,
    b_key,
    b_value,
    cache_keys,
    cache_values,
    block_lists,
    start_position,
):
    row_count = tokens.shape[0]
    query_width = w_query.shape[1]
    kv_width = w_key.shape[1]
    heads_kv = kv_width // HD
    block_count = row_count // QBLK
    widened = tokens.astype(jnp.float32)
    normed = (
        widened
        * lax.rsqrt(jnp.mean(widened * widened, axis=-1, keepdims=True) + norm_eps)
        * norm_gain.astype(jnp.float32)
    ).astype(jnp.bfloat16)
    panels = (
        lax.all_gather(w_query, "grp", axis=0, tiled=True),
        lax.all_gather(w_key, "grp", axis=0, tiled=True),
        lax.all_gather(w_value, "grp", axis=0, tiled=True),
    )
    query_lin, key_lin, value_lin = tuple(
        (jnp.dot(normed, panel, preferred_element_type=jnp.float32) for panel in panels)
    )
    row_start = (lax.axis_index("ctx") * lax.axis_size("grp") + lax.axis_index("grp")) * row_count
    positions = start_position[0] + row_start + jnp.arange(row_count, dtype=jnp.int32)
    query = rotate(
        (query_lin + b_query.astype(jnp.float32)).reshape(row_count, heads_kv * GROUP, HD),
        positions,
    )
    keys_new = rotate(
        (key_lin + b_key.astype(jnp.float32)).reshape(row_count, heads_kv, HD), positions
    ).reshape(row_count, kv_width)
    values_new = value_lin + b_value.astype(jnp.float32)
    score_scale = HD ** (-0.5)
    query_heads = query.reshape(row_count, heads_kv, GROUP, HD)
    query_blocks = query.reshape(block_count, QBLK, heads_kv, GROUP, HD)
    key_blocks = keys_new.reshape(block_count, QBLK, heads_kv, HD)
    value_blocks = values_new.reshape(block_count, QBLK, heads_kv, HD)
    near_scores = jnp.einsum("bqkgd,bskd->kgbqs", query_blocks, key_blocks) * score_scale
    causal = lax.broadcasted_iota(jnp.int32, (QBLK, QBLK), 0) >= lax.broadcasted_iota(
        jnp.int32, (QBLK, QBLK), 1
    )
    near_scores = jnp.where(causal, near_scores, -jnp.inf)
    near_max = jnp.max(near_scores, axis=-1)
    near_exp = jnp.exp(near_scores - near_max[..., None])
    near_total = jnp.sum(near_exp, axis=-1)
    near_weighted = jnp.einsum("kgbqs,bskd->kgbqd", near_exp, value_blocks)
    initial_state = (
        near_max.reshape(heads_kv, GROUP, row_count),
        near_total.reshape(heads_kv, GROUP, row_count),
        near_weighted.reshape(heads_kv, GROUP, row_count, HD),
    )
    piece_keys = lax.all_gather(cache_keys, "ctx", axis=0, tiled=True)
    piece_values = lax.all_gather(cache_values, "ctx", axis=0, tiled=True)
    key_count = piece_keys.shape[0]

    def one_key_block(block_step, state_inner):
        old_max, old_total, old_weighted = state_inner
        block_keys = (
            lax.dynamic_slice_in_dim(piece_keys, block_step * QBLK, QBLK, 0)
            .reshape(QBLK, heads_kv, HD)
            .astype(jnp.float32)
        )
        block_values = (
            lax.dynamic_slice_in_dim(piece_values, block_step * QBLK, QBLK, 0)
            .reshape(QBLK, heads_kv, HD)
            .astype(jnp.float32)
        )
        attention_affinity = jnp.einsum("rkgd,pkd->kgrp", query_heads, block_keys) * score_scale
        listed = jnp.any(block_lists == block_step, axis=2).reshape(
            heads_kv, GROUP, block_count, 1, 1
        )
        attention_affinity = jnp.where(
            listed, attention_affinity.reshape(heads_kv, GROUP, block_count, QBLK, QBLK), -jnp.inf
        ).reshape(heads_kv, GROUP, row_count, QBLK)
        new_max = jnp.maximum(old_max, jnp.max(attention_affinity, axis=-1))
        factor = jnp.exp(old_max - new_max)
        weights = jnp.exp(attention_affinity - new_max[..., None])
        new_total = old_total * factor + jnp.sum(weights, axis=-1)
        new_weighted = old_weighted * factor[..., None] + jnp.einsum(
            "kgrp,pkd->kgrd", weights, block_values
        )
        return (new_max, new_total, new_weighted)

    final_max, row_total, weighted = lax.fori_loop(
        0, key_count // QBLK, one_key_block, initial_state
    )
    context = jnp.transpose(weighted / row_total[..., None], (2, 0, 1, 3)).reshape(
        row_count, query_width
    )
    return (context, keys_new, values_new)


def solution(mesh):
    in_specs = (
        P(("ctx", "grp"), None),
        P(),
        P("grp", None),
        P("grp", None),
        P("grp", None),
        P(),
        P(),
        P(),
        P("ctx", None),
        P("ctx", None),
        P(None, ("ctx", "grp"), None),
        P(),
    )
    out_specs = (P(("ctx", "grp"), None), P(("ctx", "grp"), None), P(("ctx", "grp"), None))
    return jax.shard_map(
        on_device, mesh=mesh, in_specs=in_specs, out_specs=out_specs, check_vma=False
    )
```

profile of v0, /device:TPU:1, one launch (start us, length us, event | category | flops | bytes accessed | tf_op | source)
XLA Modules:
  0.0 523.7 jit_solution(8601297681478014044)
XLA Ops:
  9.5 1.7 copy.59
  15.4 62.1 %all-gather.6.cloned.1.call-done = bf16[2560,512]{1,0:T(8,128)(2,1)} async-done(((bf16[160,512]{1,0:T(8,128)(2,1)}), bf16[2560,512]{1,0:T(8,128)(2,1)}) %all-gather.6.cloned.1.call-update) | async-done | bytes 2621456 | tf_op jit(solution)/shard_map/all_gather | solution.py:72
  77.5 2.6 convolution_add_fusion.2
  81.2 68.9 %all-gather.10.cloned.1.call-done = bf16[2560,512]{1,0:T(8,128)(2,1)} async-done(((bf16[160,512]{1,0:T(8,128)(2,1)}), bf16[2560,512]{1,0:T(8,128)(2,1)}) %all-gather.10.cloned.1.call-update) | async-done | bytes 2621456 | tf_op jit(solution)/shard_map/all_gather | solution.py:73
  150.2 2.6 convolution_add_fusion.1
  153.8 153.8 %all-gather.8.cloned.1.call-done = bf16[2560,2560]{1,0:T(8,128)(2,1)} async-done(((bf16[160,2560]{1,0:T(8,128)(2,1)}), bf16[2560,2560]{1,0:T(8,128)(2,1)}) %all-gather.8.cloned.1.call-update) | async-done | bytes 13107216 | tf_op jit(solution)/shard_map/all_gather | solution.py:71
  307.5 9.8 %convolution_add_fusion = f32[256,2560]{1,0:T(8,128)} fusion(bf16[2560,2560]{1,0:T(8,128)(2,1)} %all-gather.8.cloned.1.call-done, f32[2560]{0:T(1024)S(1)} %convert_element_type.64, bf16[256,2560]{1,0:T(8,128)(2,1)S(1)} %copy-done.2, f32[2560]{0:T(1024)S(1)} %convert_element_type.57, f32[256]{0:T(256)S(1)} %add_rsqrt_fusion), kind=kOutput, calls=%fused_computation.17 | convolution fusion | flops 3358720000 | bytes 17060864 | tf_op jit(solution)/shard_map/dot_general | solution.py:76
  317.4 2.1 copy.52
  324.0 2.4 copy.62
  326.5 2.3 fusion.15
  328.8 34.0 %all-gather.12.cloned.1.call-done = bf16[2048,512]{0,1:T(8,128)(2,1)} async-done(((bf16[128,512]{0,1:T(8,128)(2,1)}), bf16[2048,512]{0,1:T(8,128)(2,1)}) %all-gather.12.cloned.1.call-update) | async-done | bytes 2097168 | tf_op jit(solution)/shard_map/all_gather | solution.py:107
  362.8 55.9 %all-gather.14.cloned.1.call-done = bf16[2048,512]{0,1:T(8,128)(2,1)} async-done(((bf16[128,512]{0,1:T(8,128)(2,1)}), bf16[2048,512]{0,1:T(8,128)(2,1)}) %all-gather.14.cloned.1.call-update) | async-done | bytes 2097168 | tf_op jit(solution)/shard_map/all_gather | solution.py:108
  418.7 92.3 %while.17 = (s32[]{:T(128)}, f32[4,5,256]{2,1,0:T(8,128)S(1)}, f32[4,5,256]{2,1,0:T(8,128)S(1)}, f32[4,5,256,128]{3,2,1,0:T(8,128)S(1)}, s32[20,2,4]{0,2,1:T(4,1...) while((s32[]{:T(128)}, f32[4,5,256]{2,1,0:T(8,128)S(1)}, ...), condition=%wide.region_7.8_spmd, body=%wide.region_3.7_spmd.sunk | while | flops 343419168 | bytes 15574043 | solution.py:139
  420.0 1.9 fusion.51
  422.6 1.8 multiply_add_fusion.8
  425.8 1.9 fusion.51
  428.4 1.8 multiply_add_fusion.8
  431.6 1.9 fusion.51
  434.2 1.8 multiply_add_fusion.8
  437.4 1.9 fusion.51
  439.9 1.8 multiply_add_fusion.8
  443.1 1.9 fusion.51
  445.7 1.8 multiply_add_fusion.8
  448.9 1.9 fusion.51
  451.5 1.8 multiply_add_fusion.8
  454.7 1.9 fusion.51
  457.2 1.8 multiply_add_fusion.8
  460.4 1.9 fusion.51
  463.0 1.8 multiply_add_fusion.8
  466.2 1.9 fusion.51
  468.8 1.8 multiply_add_fusion.8
  472.0 1.9 fusion.51
  474.6 1.8 multiply_add_fusion.8
  477.7 1.9 fusion.51
  480.3 1.8 multiply_add_fusion.8
  483.5 1.9 fusion.51
  486.1 1.8 multiply_add_fusion.8
  489.3 1.9 fusion.51
  491.9 1.8 multiply_add_fusion.8
  495.1 1.9 fusion.51
  497.6 1.8 multiply_add_fusion.8
  500.8 1.9 fusion.51
  503.4 1.8 multiply_add_fusion.8
  506.6 1.9 fusion.51
  509.2 1.8 multiply_add_fusion.8
  511.0 2.1 copy.63
  513.1 2.0 broadcast_divide_fusion
  515.1 2.1 copy.64
  (235 shorter events, 44.2 us)
Async XLA Ops:
  7.2 7.5 %copy-start.8 = (f32[64]{0:T(128)S(1)}, f32[64]{0:T(128)}, u32[]{:S(2)}) copy-start(f32[64]{0:T(128)} %constant.155) | copy-start | bytes 772
  7.2 7.5 %copy-start.9 = (f32[64]{0:T(128)S(1)}, f32[64]{0:T(128)}, u32[]{:S(2)}) copy-start(f32[64]{0:T(128)} %constant.157) | copy-start | bytes 772
  7.2 7.5 %copy-start.10 = (f32[64]{0:T(128)S(1)}, f32[64]{0:T(128)}, u32[]{:S(2)}) copy-start(f32[64]{0:T(128)} %constant.159) | copy-start | bytes 772
  7.2 7.5 %copy-start.11 = (f32[64]{0:T(128)S(1)}, f32[64]{0:T(128)}, u32[]{:S(2)}) copy-start(f32[64]{0:T(128)} %constant.161) | copy-start | bytes 772
  7.2 7.1 %copy-start.2 = (bf16[256,2560]{1,0:T(8,128)(2,1)S(1)}, bf16[256,2560]{1,0:T(8,128)(2,1)}, u32[]{:S(2)}) copy-start(bf16[256,2560]{1,0:T(8,128)(2,1)} %param.16) | copy-start | bytes 3932164
  7.2 7.5 %copy-start.5 = (bf16[2560]{0:T(1024)(128)(2,1)S(1)}, bf16[2560]{0:T(1024)(128)(2,1)}, u32[]{:S(2)}) copy-start(bf16[2560]{0:T(1024)(128)(2,1)} %param.21) | copy-start | bytes 15364
  7.2 8.1 %copy-start.6 = (bf16[512]{0:T(512)(128)(2,1)S(1)}, bf16[512]{0:T(512)(128)(2,1)}, u32[]{:S(2)}) copy-start(bf16[512]{0:T(512)(128)(2,1)} %param.22) | copy-start | bytes 3076
  7.2 8.1 %copy-start.7 = (bf16[512]{0:T(512)(128)(2,1)S(1)}, bf16[512]{0:T(512)(128)(2,1)}, u32[]{:S(2)}) copy-start(bf16[512]{0:T(512)(128)(2,1)} %param.23) | copy-start | bytes 3076
  7.3 70.2 %all-gather.6.cloned.1.call-start = ((), (), s32[]{:S(2)}) async-start(), calls=%async_computation | async-start | bytes 2785280 | tf_op jit(solution)/shard_map/all_gather | solution.py:72
  8.0 142.2 %all-gather.10.cloned.1.call-start = ((), (), s32[]{:S(2)}) async-start(), calls=%async_computation.2 | async-start | bytes 2785280 | tf_op jit(solution)/shard_map/all_gather | solution.py:73
  8.7 298.8 %all-gather.8.cloned.1.call-start = ((), (), s32[]{:S(2)}) async-start(), calls=%async_computation.1 | async-start | bytes 13926400 | tf_op jit(solution)/shard_map/all_gather | solution.py:71
  9.5 353.3 %all-gather.12.cloned.1.call-start = ((), (), s32[]{:S(2)}) async-start(), calls=%async_computation.3 | async-start | bytes 2228224 | tf_op jit(solution)/shard_map/all_gather | solution.py:107
  11.2 407.5 %all-gather.14.cloned.1.call-start = ((), (), s32[]{:S(2)}) async-start(), calls=%async_computation.4 | async-start | bytes 2228224 | tf_op jit(solution)/shard_map/all_gather | solution.py:108
  152.8 154.7 %copy-start.3 = (f32[256,512]{1,0:T(8,128)}, f32[256,512]{1,0:T(8,128)S(1)}, u32[]{:S(2)}) copy-start(f32[256,512]{1,0:T(8,128)S(1)} %convolution_add_fusion.1) | copy-start | bytes 1572868
  320.0 1.4 copy-start.1
  321.4 1.5 copy-start
  324.0 94.6 %copy-start.4 = (s32[20,2,4]{0,2,1:T(4,128)S(1)}, s32[20,2,4]{0,2,1:T(4,128)}, u32[]{:S(2)}) copy-start(s32[20,2,4]{0,2,1:T(4,128)} %param.26) | copy-start | bytes 1924
Sparse Core Ops, SparseCore 0:
  9.9 67.5 all-gather.5
  79.3 70.8 all-gather.9
  152.0 155.5 all-gather.7
  309.9 52.7 all-gather.11
  365.1 53.4 all-gather.13
where the time goes:
time: 525 us; the launch traced here: 524 us
  waiting for transfers between devices  377 us (72%)
  matrix products  75.4 us (14%)
  local copies, waits for them, and re-layouts  37.5 us (7%)
  other arithmetic  17.8 us (3%)
  between operations  14.8 us (3%)
    all_gather x1, waiting for transfers between devices, on_device(): lax.all_gather(w_query, 'grp', axis=0, tiled=True)  154 us
    all_gather x1, waiting for transfers between devices, on_device(): lax.all_gather(w_value, 'grp', axis=0, tiled=True)  68.9 us
    all_gather x1, waiting for transfers between devices, on_device(): lax.all_gather(w_key, 'grp', axis=0, tiled=True)  62.1 us
    all_gather x1, waiting for transfers between devices, on_device(): piece_values = lax.all_gather(cache_values, 'ctx', axis=0, tiled=True)  55.9 us
    all_gather x1, waiting for transfers between devices, on_device(): piece_keys = lax.all_gather(cache_keys, 'ctx', axis=0, tiled=True)  34 us
    dot_general x16, matrix products, one_key_block(): jnp.einsum('rkgd,pkd->kgrp', query_heads, block_keys) * score_scale  30.5 us
    dot_general x16, matrix products, one_key_block(): jnp.einsum('kgrp,pkd->kgrd', weights, block_values)  28.4 us
    dynamic_slice x16, local copies, waits for them, and re-layouts, one_key_block(): lax.dynamic_slice_in_dim(piece_values, block_step * QBLK, QBLK, 0)  15.9 us
  transfers between devices with their start and end apart: 5, of which 5 were waited for; matrix products, arithmetic and copies ran while one was open for 6% of the time, Pallas kernels for 0%

commit v1 on v0

--- a/solution.py
+++ b/solution.py
@@ -3,6 +3,7 @@
 import numpy as np
 from jax import lax
 from jax.sharding import PartitionSpec as P
+from jax.lax import all_to_all, axis_size
 
 HD = 128
 GROUP = 5
@@ -70,7 +71,10 @@
     panels = (
         lax.all_gather(w_query, "grp", axis=0, tiled=True),
         lax.all_gather(w_key, "grp", axis=0, tiled=True),
-        lax.all_gather(w_value, "grp", axis=0, tiled=True),
+        jnp.concatenate(
+            all_to_all(jnp.stack([w_value for _ in range(axis_size("grp"))], axis=0), "grp", 0, 0),
+            axis=0,
+        ),
     )
     query_lin, key_lin, value_lin = tuple(
         (jnp.dot(normed, panel, preferred_element_type=jnp.float32) for panel in panels)

time: 525 us -> 489 us (0.931)
  waiting for transfers between devices: 377 us -> 323 us
  starting transfers between devices: 0.19 us -> 10.4 us
    all_gather x1 -> x0, waiting for transfers between devices: 68.9 us -> none  [on_device(): lax.all_gather(w_value, 'grp', axis=0, tiled=True)]
    all_gather x1, waiting for transfers between devices: 62.1 us -> 90.5 us  [on_device(): lax.all_gather(w_key, 'grp', axis=0, tiled=True)]
    all_gather x1, waiting for transfers between devices: 55.9 us -> 33.7 us  [on_device(): piece_values = lax.all_gather(cache_values, 'ctx', axis=0, tiled=True)]
    all_gather x1, waiting for transfers between devices: 34 us -> 55.9 us  [on_device(): piece_keys = lax.all_gather(cache_keys, 'ctx', axis=0, tiled=True)]
    all_gather x1, waiting for transfers between devices: 154 us -> 141 us  [on_device(): lax.all_gather(w_query, 'grp', axis=0, tiled=True)]
    all_to_all x0 -> x1, starting transfers between devices: none -> 10.3 us  [on_device(): all_to_all(jnp.stack([w_value for _ in range(axis_size('grp'))], axis=0),...]
  transfers between devices with their start and end apart: 5 -> 5, of which waited for: 5 -> 4; matrix products, arithmetic and copies ran while one was open for 6% -> 8% of each run, Pallas kernels for 0% -> 0%
where the time goes in v1:
time: 489 us; the launch traced here: 488 us
  waiting for transfers between devices  323 us (66%)
  matrix products  77.4 us (16%)
  local copies, waits for them, and re-layouts  41.3 us (8%)
  other arithmetic  19.6 us (4%)
  between operations  14.7 us (3%)
  starting transfers between devices  10.4 us (2%)
    all_gather x1, waiting for transfers between devices, on_device(): lax.all_gather(w_query, 'grp', axis=0, tiled=True)  141 us
    all_gather x1, waiting for transfers between devices, on_device(): lax.all_gather(w_key, 'grp', axis=0, tiled=True)  90.5 us
    all_gather x1, waiting for transfers between devices, on_device(): piece_keys = lax.all_gather(cache_keys, 'ctx', axis=0, tiled=True)  55.9 us
    all_gather x1, waiting for transfers between devices, on_device(): piece_values = lax.all_gather(cache_values, 'ctx', axis=0, tiled=True)  33.7 us
    dot_general x16, matrix products, one_key_block(): jnp.einsum('rkgd,pkd->kgrp', query_heads, block_keys) * score_scale  30.5 us
    dot_general x16, matrix products, one_key_block(): jnp.einsum('kgrp,pkd->kgrd', weights, block_values)  28.4 us
    dot_general x3, matrix products, on_device(): jnp.dot(normed, panel, preferred_element_type=jnp.float32)  17 us
    dynamic_slice x16, local copies, waits for them, and re-layouts, one_key_block(): lax.dynamic_slice_in_dim(piece_values, block_step * QBLK, QBLK, 0)  15.9 us
  transfers between devices with their start and end apart: 5, of which 4 were waited for; matrix products, arithmetic and copies ran while one was open for 8% of the time, Pallas kernels for 0%

profile of v1, /device:TPU:1, one launch (start us, length us, event | category | flops | bytes accessed | tf_op | source)
XLA Modules:
  0.0 487.8 jit_solution(14242825358918190129)
XLA Ops:
  10.4 2.7 stack.2
  13.1 10.3 %all-to-all-start = ((bf16[16,160,512]{2,1,0:T(8,128)(2,1)}), bf16[16,160,512]{2,1,0:T(8,128)(2,1)S(1)}, u32[]{:S(2)}, u32[]{:S(2)}) async-start(bf16[16,160,512]{2,1,0:T(8,128)(2,1)} %stack.2), calls=%async_computation | async-start | bytes 5242880 | tf_op jit(solution)/shard_map/all_to_all | solution.py:75
  28.5 90.5 %all-gather.5.cloned.1.call-done = bf16[2560,512]{1,0:T(8,128)(2,1)} async-done(((bf16[160,512]{1,0:T(8,128)(2,1)}), bf16[2560,512]{1,0:T(8,128)(2,1)}) %all-gather.5.cloned.1.call-update) | async-done | bytes 2621456 | tf_op jit(solution)/shard_map/all_gather | solution.py:73
  119.0 3.8 convolution_add_fusion.2
  125.0 3.0 convolution_add_fusion.1
  129.9 141.5 %all-gather.7.cloned.1.call-done = bf16[2560,2560]{1,0:T(8,128)(2,1)} async-done(((bf16[160,2560]{1,0:T(8,128)(2,1)}), bf16[2560,2560]{1,0:T(8,128)(2,1)}) %all-gather.7.cloned.1.call-update) | async-done | bytes 13107216 | tf_op jit(solution)/shard_map/all_gather | solution.py:72
  271.4 10.2 %convolution_add_fusion = f32[256,2560]{1,0:T(8,128)} fusion(bf16[2560,2560]{1,0:T(8,128)(2,1)} %all-gather.7.cloned.1.call-done, f32[2560]{0:T(1024)} %convert_element_type.64, bf16[256,2560]{1,0:T(8,128)(2,1)} %param.16, f32[2560]{0:T(1024)} %copy-done.4, f32[256]{0:T(256)} %copy-done.9), kind=kOutput, calls=%fused_computation.17 | convolution fusion | flops 3358720000 | bytes 17060864 | tf_op jit(solution)/shard_map/dot_general | solution.py:80
  281.6 2.1 copy.52
  288.3 2.4 copy.62
  290.7 2.3 fusion.15
  293.0 33.7 %all-gather.11.cloned.1.call-done = bf16[2048,512]{0,1:T(8,128)(2,1)} async-done(((bf16[128,512]{0,1:T(8,128)(2,1)}), bf16[2048,512]{0,1:T(8,128)(2,1)}) %all-gather.11.cloned.1.call-update) | async-done | bytes 2097168 | tf_op jit(solution)/shard_map/all_gather | solution.py:112
  326.8 55.9 %all-gather.9.cloned.1.call-done = bf16[2048,512]{0,1:T(8,128)(2,1)} async-done(((bf16[128,512]{0,1:T(8,128)(2,1)}), bf16[2048,512]{0,1:T(8,128)(2,1)}) %all-gather.9.cloned.1.call-update) | async-done | bytes 2097168 | tf_op jit(solution)/shard_map/all_gather | solution.py:111
  382.7 92.3 %while.17 = (s32[]{:T(128)}, f32[4,5,256]{2,1,0:T(8,128)S(1)}, f32[4,5,256]{2,1,0:T(8,128)S(1)}, f32[4,5,256,128]{3,2,1,0:T(8,128)S(1)}, s32[20,2,4]{0,2,1:T(4,1...) while((s32[]{:T(128)}, f32[4,5,256]{2,1,0:T(8,128)S(1)}, ...), condition=%wide.region_7.8_spmd, body=%wide.region_3.7_spmd.sunk | while | flops 343419168 | bytes 15574043 | solution.py:143
  384.1 1.9 fusion.51
  386.6 1.8 multiply_add_fusion.8
  389.8 1.9 fusion.51
  392.4 1.8 multiply_add_fusion.8
  395.6 1.9 fusion.51
  398.2 1.8 multiply_add_fusion.8
  401.4 1.9 fusion.51
  403.9 1.8 multiply_add_fusion.8
  407.1 1.9 fusion.51
  409.7 1.8 multiply_add_fusion.8
  412.9 1.9 fusion.51
  415.5 1.8 multiply_add_fusion.8
  418.7 1.9 fusion.51
  421.3 1.8 multiply_add_fusion.8
  424.5 1.9 fusion.51
  427.0 1.8 multiply_add_fusion.8
  430.2 1.9 fusion.51
  432.8 1.8 multiply_add_fusion.8
  436.0 1.9 fusion.51
  438.6 1.8 multiply_add_fusion.8
  441.8 1.9 fusion.51
  444.4 1.8 multiply_add_fusion.8
  447.5 1.9 fusion.51
  450.1 1.8 multiply_add_fusion.8
  453.3 1.9 fusion.51
  455.9 1.8 multiply_add_fusion.8
  459.1 1.9 fusion.51
  461.7 1.8 multiply_add_fusion.8
  464.9 1.9 fusion.51
  467.4 1.8 multiply_add_fusion.8
  470.6 1.9 fusion.51
  473.2 1.8 multiply_add_fusion.8
  475.0 2.1 copy.63
  477.1 2.0 broadcast_divide_fusion
  479.1 2.1 copy.64
  (239 shorter events, 48.0 us)
Async XLA Ops:
  7.2 111.8 %all-gather.5.cloned.1.call-start = ((), (), s32[]{:S(2)}) async-start(), calls=%async_computation.1 | async-start | bytes 2785280 | tf_op jit(solution)/shard_map/all_gather | solution.py:73
  7.9 263.5 %all-gather.7.cloned.1.call-start = ((), (), s32[]{:S(2)}) async-start(), calls=%async_computation.2 | async-start | bytes 13926400 | tf_op jit(solution)/shard_map/all_gather | solution.py:72
  8.6 318.1 %all-gather.11.cloned.1.call-start = ((), (), s32[]{:S(2)}) async-start(), calls=%async_computation.4 | async-start | bytes 2228224 | tf_op jit(solution)/shard_map/all_gather | solution.py:112
  13.0 10.4 %copy-start.2 = (bf16[128,512]{1,0:T(8,128)(2,1)S(1)}, bf16[128,512]{1,0:T(8,128)(2,1)}, u32[]{:S(2)}) copy-start(bf16[128,512]{1,0:T(8,128)(2,1)} %param.24) | copy-start | bytes 393220
  13.0 11.8 %copy-start.5 = (bf16[2560]{0:T(1024)(128)(2,1)S(1)}, bf16[2560]{0:T(1024)(128)(2,1)}, u32[]{:S(2)}) copy-start(bf16[2560]{0:T(1024)(128)(2,1)} %param.17) | copy-start | bytes 15364
  13.0 11.9 %copy-start.6 = (bf16[2560]{0:T(1024)(128)(2,1)S(1)}, bf16[2560]{0:T(1024)(128)(2,1)}, u32[]{:S(2)}) copy-start(bf16[2560]{0:T(1024)(128)(2,1)} %param.21) | copy-start | bytes 15364
  13.1 12.5 %copy-start.10 = (f32[64]{0:T(128)S(1)}, f32[64]{0:T(128)}, u32[]{:S(2)}) copy-start(f32[64]{0:T(128)} %constant.155) | copy-start | bytes 772
  13.1 12.5 %copy-start.11 = (f32[64]{0:T(128)S(1)}, f32[64]{0:T(128)}, u32[]{:S(2)}) copy-start(f32[64]{0:T(128)} %constant.157) | copy-start | bytes 772
  13.1 12.5 %copy-start.12 = (f32[64]{0:T(128)S(1)}, f32[64]{0:T(128)}, u32[]{:S(2)}) copy-start(f32[64]{0:T(128)} %constant.159) | copy-start | bytes 772
  13.1 12.5 %copy-start.13 = (f32[64]{0:T(128)S(1)}, f32[64]{0:T(128)}, u32[]{:S(2)}) copy-start(f32[64]{0:T(128)} %constant.161) | copy-start | bytes 772
  13.1 13.1 %copy-start.7 = (bf16[512]{0:T(512)(128)(2,1)S(1)}, bf16[512]{0:T(512)(128)(2,1)}, u32[]{:S(2)}) copy-start(bf16[512]{0:T(512)(128)(2,1)} %param.22) | copy-start | bytes 3076
  13.1 13.1 %copy-start.8 = (bf16[512]{0:T(512)(128)(2,1)S(1)}, bf16[512]{0:T(512)(128)(2,1)}, u32[]{:S(2)}) copy-start(bf16[512]{0:T(512)(128)(2,1)} %param.23) | copy-start | bytes 3076
  13.1 111.8 %all-to-all-start = ((bf16[16,160,512]{2,1,0:T(8,128)(2,1)}), bf16[16,160,512]{2,1,0:T(8,128)(2,1)S(1)}, u32[]{:S(2)}, u32[]{:S(2)}) async-start(bf16[16,160,512]{2,1,0:T(8,128)(2,1)} %stack.2), calls=%async_computation | async-start | bytes 5242880 | tf_op jit(solution)/shard_map/all_to_all | solution.py:75
  23.4 359.3 %all-gather.9.cloned.1.call-start = ((), (), s32[]{:S(2)}) async-start(), calls=%async_computation.3 | async-start | bytes 2228224 | tf_op jit(solution)/shard_map/all_gather | solution.py:111
  24.9 94.0 %copy-start.4 = (f32[2560]{0:T(1024)}, f32[2560]{0:T(1024)S(1)}, u32[]{:S(2)}) copy-start(f32[2560]{0:T(1024)S(1)} %convert_element_type.57) | copy-start | bytes 30724
  28.5 90.5 %copy-start.9 = (f32[256]{0:T(256)}, f32[256]{0:T(256)S(1)}, u32[]{:S(2)}) copy-start(f32[256]{0:T(256)S(1)} %add_rsqrt_fusion) | copy-start | bytes 3076
  284.2 1.4 copy-start.1
  285.6 1.5 copy-start
  288.2 94.4 %copy-start.3 = (s32[20,2,4]{0,2,1:T(4,128)S(1)}, s32[20,2,4]{0,2,1:T(4,128)}, u32[]{:S(2)}) copy-start(s32[20,2,4]{0,2,1:T(4,128)} %param.26) | copy-start | bytes 1924
Sparse Core Ops, SparseCore 0:
  9.8 109.1 all-gather.4
  120.7 150.6 all-gather.6
  274.0 52.7 all-gather.10
  329.2 53.4 all-gather.8
